TPU v7x, 128 devices: a whole 4x4x4 slice. The times are simulated.
128 devices in a mesh: fsdp: 16 (over y, z_hi, core), sp: 8 (over z_lo, x).
Axes of the slice: x: 4, y: 4, z: 4 (z_hi: 2, z_lo: 2; z = z_hi * 2 + z_lo), core: 2. Of those that a mesh axis runs over, the one named last changes fastest.
Arguments:
- tokens: bfloat16 [16384, 5120], P(('fsdp', 'sp')), may hold values from -6 to 6
- norm_gain: float32 [5120], replicated, may hold values from 0.1 to 1.9
- q_weight: bfloat16 [5120, 5120], P('fsdp', 'sp'), may hold values from -0.078125 to 0.078125
- key_matrix: bfloat16 [5120, 1024], P('fsdp', 'sp'), may hold values from -0.078125 to 0.078125
- value_matrix: bfloat16 [5120, 1024], P('fsdp', 'sp'), may hold values from -0.078125 to 0.078125
- q_bias: float32 [5120], P('sp'), may hold values from -8 to 8
- k_bias: float32 [1024], P('sp'), may hold values from -8 to 8
- value_offset_bias: float32 [1024], P('sp'), may hold values from -3 to 3
- out_weight: bfloat16 [5120, 5120], P('fsdp', 'sp'), may hold values from -0.078125 to 0.078125
Outputs:
- mixed: bfloat16 [16384, 5120], P(('fsdp', 'sp'))
All inputs are finite; a program needn't handle non-finite values.
Results may differ from a plain program's by a relative error of at most 0.014.
Values may be sent and summed in bfloat16 or wider, within the bound.
A program may use at most 128 MiB of HBM per device.

v0:
```python
import jax
import jax.numpy as jnp
from jax import lax
from jax.sharding import PartitionSpec as P

HEAD_SIZE = 128


ROPE_BASE = 1000000.0


def rms_normed(tokens, norm_gain):
    rows = tokens.astype(jnp.float32)
    meansq = jnp.mean(rows * rows, axis=-1, keepdims=True)
    return (rows * lax.rsqrt(meansq + 1e-06) * norm_gain).astype(jnp.bfloat16)


def rotary(projected, positions):
    count = projected.shape[0]
    heads_grid = projected.reshape(count, -1, HEAD_SIZE)
    half_dim = HEAD_SIZE // 2
    frequency = ROPE_BASE ** (-(jnp.arange(half_dim, dtype=jnp.float32) * 2.0 / HEAD_SIZE))
    angle = positions[:, None] * frequency[None, :]
    cosine = jnp.cos(angle)[:, None, :]
    sine = jnp.sin(angle)[:, None, :]
    first = heads_grid[..., :half_dim]
    second = heads_grid[..., half_dim:]
    rotated = jnp.concatenate(
        [first * cosine - second * sine, second * cosine + first * sine], axis=-1
    )
    return rotated.reshape(count, -1)


def attend(queries, keys, values):
    length = queries.shape[0]
    kv_heads = keys.shape[1] // HEAD_SIZE
    group_size = queries.shape[1] // keys.shape[1]
    query_grid = queries.reshape(length, kv_heads, group_size, HEAD_SIZE)
    key_grid = keys.reshape(length, kv_heads, HEAD_SIZE)
    value_grid = values.reshape(length, kv_heads, HEAD_SIZE)
    scores = jnp.einsum(
        "qkgd,skd->kgqs", query_grid, key_grid, preferred_element_type=jnp.float32
    ) / jnp.sqrt(jnp.float32(HEAD_SIZE))
    causal = lax.iota(jnp.int32, length)[:, None] >= lax.iota(jnp.int32, length)[None, :]
    scores = jnp.where(causal, scores, jnp.float32(-1e30))
    largest = jnp.max(scores, axis=-1, keepdims=True)
    weights = jnp.exp(scores - largest)
    totals = jnp.sum(weights, axis=-1, keepdims=True)
    probs = (weights / totals).astype(jnp.bfloat16)
    result = jnp.einsum("kgqs,skd->qkgd", probs, value_grid, preferred_element_type=jnp.float32)
    return result.reshape(length, -1).astype(jnp.bfloat16)


def project_heads(normed, q_full, k_full, v_full, q_bias, k_bias, value_offset_bias):
    q_cols = q_full.shape[1]
    k_cols = k_full.shape[1]
    piece = lax.all_gather(normed, "sp", axis=0, tiled=True)
    count = piece.shape[0]
    positions = lax.iota(jnp.int32, count).astype(jnp.float32)
    queries = rotary(jnp.dot(piece, q_full, preferred_element_type=jnp.float32) + q_bias, positions)
    keys = rotary(jnp.dot(piece, k_full, preferred_element_type=jnp.float32) + k_bias, positions)
    values = jnp.dot(piece, v_full, preferred_element_type=jnp.float32) + value_offset_bias
    stacked = jnp.concatenate([queries, keys, values], axis=1).astype(jnp.bfloat16)
    queries = stacked[:, :q_cols]
    keys = stacked[:, q_cols : q_cols + k_cols]
    values = stacked[:, q_cols + k_cols :]
    return attend(queries, keys, values)


def body(
    tokens,
    norm_gain,
    q_weight,
    key_matrix,
    value_matrix,
    q_bias,
    k_bias,
    value_offset_bias,
    out_weight,
):
    normed = rms_normed(tokens, norm_gain)
    q_full, k_full, v_full = (
        lax.all_gather(q_weight, "fsdp", axis=0, tiled=True),
        lax.all_gather(key_matrix, "fsdp", axis=0, tiled=True),
        lax.all_gather(value_matrix, "fsdp", axis=0, tiled=True),
    )
    heads = project_heads(normed, q_full, k_full, v_full, q_bias, k_bias, value_offset_bias)
    partial_value = lax.dot_general(
        heads,
        lax.all_gather(out_weight, "fsdp", axis=0, tiled=True),
        (((1,), (1,)), ((), ())),
        preferred_element_type=jnp.float32,
    )
    mixed = lax.psum_scatter(
        partial_value.astype(jnp.bfloat16), "sp", scatter_dimension=0, tiled=True
    )
    return mixed


def solution(mesh):
    placed = (
        P(("fsdp", "sp"), None),
        P(),
        P("fsdp", "sp"),
        P("fsdp", "sp"),
        P("fsdp", "sp"),
        P("sp"),
        P("sp"),
        P("sp"),
        P("fsdp", "sp"),
    )
    return jax.shard_map(
        body, mesh=mesh, in_specs=placed, out_specs=P(("fsdp", "sp"), None), check_vma=False
    )
```

profile of v0, /device:TPU:1, one launch (start us, length us, event | category | flops | bytes accessed | tf_op | source)
XLA Modules:
  0.0 480.5 jit_solution(17272657768268774551)
XLA Ops:
  6.5 0.0 copy-start.2
  6.5 0.0 all-gather.12.cloned.1.call-start
  6.5 0.7 all-gather.12.cloned.1.call-update
  7.3 0.0 all-gather.6.cloned.1.call-start
  7.3 1.7 fusion.4
  9.0 0.0 copy-done.2
  9.0 2.2 fusion.6
  11.2 0.0 copy-start.6
  11.2 0.0 all-gather.6.cloned.1.call-update
  11.2 0.0 all-gather.10.cloned.1.call-start
  11.2 0.7 all-gather.10.cloned.1.call-update
  11.9 0.0 all-gather.8.cloned.1.call-start
  12.0 0.5 all-gather.8.cloned.1.call-update
  12.5 0.0 all-gather.14.cloned.1.call-start
  12.5 0.5 all-gather.14.cloned.1.call-update
  13.1 0.0 reduce-scatter.2.cloned.1.call-start
  13.2 1.3 iota_compare_fusion
  14.5 3.0 multiply_cosine_fusion
  17.4 60.9 %all-gather.12.cloned.1.call-done = bf16[5120,640]{1,0:T(8,128)(2,1)} async-done(((bf16[320,640]{1,0:T(8,128)(2,1)}), bf16[5120,640]{1,0:T(8,128)(2,1)}) %all-gather.12.cloned.1.call-update) | async-done | bytes 6553616 | tf_op jit(solution)/shard_map/all_gather | solution.py:83
  78.4 110.9 %all-gather.6.cloned.1.call-done = bf16[1024,5120]{1,0:T(8,128)(2,1)} async-done(((bf16[128,5120]{1,0:T(8,128)(2,1)}), bf16[1024,5120]{1,0:T(8,128)(2,1)}) %all-gather.6.cloned.1.call-update) | async-done | bytes 10485776 | tf_op jit(solution)/shard_map/all_gather | solution.py:57
  189.3 0.0 copy-done.6
  189.3 11.6 %convolution_add_fusion = f32[1024,640]{0,1:T(8,128)S(1)} fusion(bf16[1024,5120]{1,0:T(8,128)(2,1)} %all-gather.6.cloned.1.call-done, bf16[5120,640]{1,0:T(8,128)(2,1)} %all-gather.12.cloned.1.call-done, f32[640]{0:T(1024)S(1)} %copy-done.6), kind=kOutput, calls=%fused_computation.16 | convolution fusion | flops 6711541760 | bytes 19663360 | tf_op jit(solution)/shard_map/dot_general | solution.py:60
  200.9 1.8 fusion.31
  202.8 1.9 copy.17
  204.7 0.0 copy-start.5
  204.7 3.0 copy.18
  207.7 29.0 %all-gather.10.cloned.1.call-done = bf16[5120,128]{1,0:T(8,128)(2,1)} async-done(((bf16[320,128]{1,0:T(8,128)(2,1)}), bf16[5120,128]{1,0:T(8,128)(2,1)}) %all-gather.10.cloned.1.call-update) | async-done | bytes 1310736 | tf_op jit(solution)/shard_map/all_gather | solution.py:84
  236.8 0.0 copy-done.5
  236.8 0.0 copy-start.1
  236.8 0.0 copy-start.4
  236.8 8.0 %fusion.14 = f32[1024,1,128]{0,2,1:T(8,128)S(1)} fusion(bf16[1024,5120]{1,0:T(8,128)(2,1)} %all-gather.6.cloned.1.call-done, bf16[5120,128]{1,0:T(8,128)(2,1)} %all-gather.10.cloned.1.call-done, f32[128]{0:T(128)S(1)} %copy-done.5), kind=kOutput, calls=%fused_computation.23 | convolution fusion | flops 1342308352 | bytes 12321280 | tf_op jit(solution)/shard_map/dot_general | solution.py:61
  244.8 1.2 fusion.22
  246.0 0.0 copy-done.1
  246.0 0.0 copy-done.4
  246.0 2.2 subtract_convert_fusion
  248.2 0.0 copy-start.3
  248.2 6.4 %fusion.1 = (f32[5,1024]{1,0:T(8,128)S(1)}, f32[1024,1024,5]{1,0,2:T(8,128)S(1)}) fusion(pred[1024,1024]{0,1:T(8,128)(4,1)} %iota_compare_fusion, bf16[1024,5,64]{2,0,1:T(8,128)(2,1)} %get-tuple-element.6, bf16[1024,5,64]{2,0,1:T(8,128)(2,1)} %get-tuple-element.5, bf16[1024,1,64]{0,2,1:T(8,128)(2,1)S(1)} %get-tuple-element.10, ...), kind=kOutput, calls=%fused_computation.4 | convolution fusion | flops 1361046528 | bytes 23613440 | tf_op jit(solution)/shard_map/qkgd,skd->kgqs/dot_general | solution.py:41
  254.6 0.0 copy-start
  254.6 7.0 %copy-done = f32[1024,1024,5]{1,0,2:T(8,128)} copy-done((f32[1024,1024,5]{1,0,2:T(8,128)}, f32[1024,1024,5]{1,0,2:T(8,128)S(1)}, u32[]{:S(2)}) %copy-start) | copy-done | bytes 20971544
  261.6 0.0 copy-done.3
  261.6 0.0 copy-start.7
  261.6 4.8 fusion
  266.3 17.1 %all-gather.8.cloned.1.call-done = bf16[5120,128]{1,0:T(8,128)(2,1)} async-done(((bf16[320,128]{1,0:T(8,128)(2,1)}), bf16[5120,128]{1,0:T(8,128)(2,1)}) %all-gather.8.cloned.1.call-update) | async-done | bytes 1310736 | tf_op jit(solution)/shard_map/all_gather | solution.py:85
  283.4 0.0 copy-done.7
  283.4 16.2 %fusion.7 = bf16[128,5,1024]{2,0,1:T(8,128)(2,1)S(1)} fusion(f32[5,1024]{1,0:T(8,128)S(1)} %fusion, f32[5,1024]{1,0:T(8,128)S(1)} %get-tuple-element.13, f32[1024,1024,5]{1,0,2:T(8,128)} %copy-done, pred[1024,1024]{0,1:T(8,128)(4,1)S(1)} %copy-done.3, bf16[1024,5120]{1,0:T(8,128)(2,1)} %all-gather.6.cloned.1.call-done, ...), kind=kOutput, calls=%fused_computation.17 | convolution fusion | flops 2711486464 | bytes 35168768 | tf_op jit(solution)/shard_map/kgqs,skd->qkgd/dot_general | solution.py:50
  299.6 49.7 %all-gather.14.cloned.1.call-done = bf16[5120,640]{1,0:T(8,128)(2,1)} async-done(((bf16[320,640]{1,0:T(8,128)(2,1)}), bf16[5120,640]{1,0:T(8,128)(2,1)}) %all-gather.14.cloned.1.call-update) | async-done | bytes 6553616 | tf_op jit(solution)/shard_map/all_gather | solution.py:90
  349.3 13.8 %convolution_convert_fusion = bf16[1024,5120]{1,0:T(8,128)(2,1)} fusion(bf16[1024,640]{0,1:T(8,128)(2,1)S(1)} %bitcast.48, bf16[5120,640]{1,0:T(8,128)(2,1)} %all-gather.14.cloned.1.call-done), kind=kOutput, calls=%fused_computation.7 | convolution fusion | flops 6716129280 | bytes 18350080 | tf_op jit(solution)/shard_map/dot_general | solution.py:88
  363.2 0.0 reduce-scatter.2.cloned.1.call-update
  363.2 110.5 %reduce-scatter.2.cloned.1.call-done = bf16[128,5120]{1,0:T(8,128)(2,1)} async-done(((bf16[1024,5120]{1,0:T(8,128)(2,1)}), bf16[128,5120]{1,0:T(8,128)(2,1)}) %reduce-scatter.2.cloned.1.call-update) | async-done | bytes 1310736 | tf_op jit(solution)/shard_map/reduce_scatter | solution.py:94
  (3 shorter events, 0.0 us)
Async XLA Ops:
  6.5 2.4 copy-start.2
  6.5 71.8 %all-gather.12.cloned.1.call-start = ((), (), s32[]{:S(2)}) async-start(), calls=%async_computation.4 | async-start | bytes 6963200 | tf_op jit(solution)/shard_map/all_gather | solution.py:83
  7.3 182.0 %all-gather.6.cloned.1.call-start = ((), (), s32[]{:S(2)}) async-start(), calls=%async_computation.1 | async-start | bytes 11796480 | tf_op jit(solution)/shard_map/all_gather | solution.py:57
  11.2 178.1 %copy-start.6 = (f32[640]{0:T(1024)S(1)}, f32[640]{0:T(1024)}, u32[]{:S(2)}) copy-start(f32[640]{0:T(1024)} %param.14) | copy-start | bytes 7684
  11.2 225.6 %all-gather.10.cloned.1.call-start = ((), (), s32[]{:S(2)}) async-start(), calls=%async_computation.3 | async-start | bytes 1392640 | tf_op jit(solution)/shard_map/all_gather | solution.py:84
  11.9 271.5 %all-gather.8.cloned.1.call-start = ((), (), s32[]{:S(2)}) async-start(), calls=%async_computation.2 | async-start | bytes 1392640 | tf_op jit(solution)/shard_map/all_gather | solution.py:85
  12.5 336.8 %all-gather.14.cloned.1.call-start = ((), (), s32[]{:S(2)}) async-start(), calls=%async_computation.5 | async-start | bytes 6963200 | tf_op jit(solution)/shard_map/all_gather | solution.py:90
  13.1 460.6 %reduce-scatter.2.cloned.1.call-start = ((), (), s32[]{:S(2)}) async-start(), calls=%async_computation.6 | async-start | bytes 11796480 | tf_op jit(solution)/shard_map/reduce_scatter | solution.py:94
  204.7 32.1 %copy-start.5 = (f32[128]{0:T(128)S(1)}, f32[128]{0:T(128)}, u32[]{:S(2)}) copy-start(f32[128]{0:T(128)} %param.15) | copy-start | bytes 1540
  236.8 9.2 %copy-start.1 = (f32[1024,5,64]{2,0,1:T(8,128)S(1)}, f32[1024,5,64]{2,0,1:T(8,128)}, u32[]{:S(2)}) copy-start(f32[1024,5,64]{2,0,1:T(8,128)} %copy.18) | copy-start | bytes 3932164
  236.8 9.2 %copy-start.4 = (f32[1024,64]{1,0:T(8,128)S(1)}, f32[1024,64]{1,0:T(8,128)}, u32[]{:S(2)}) copy-start(f32[1024,64]{1,0:T(8,128)} %get-tuple-element.12) | copy-start | bytes 786436
  248.2 13.4 %copy-start.3 = (pred[1024,1024]{0,1:T(8,128)(4,1)S(1)}, pred[1024,1024]{0,1:T(8,128)(4,1)}, u32[]{:S(2)}) copy-start(pred[1024,1024]{0,1:T(8,128)(4,1)} %iota_compare_fusion) | copy-start | bytes 3145732
  254.6 7.0 %copy-start = (f32[1024,1024,5]{1,0,2:T(8,128)}, f32[1024,1024,5]{1,0,2:T(8,128)S(1)}, u32[]{:S(2)}) copy-start(f32[1024,1024,5]{1,0,2:T(8,128)S(1)} %get-tuple-element.14) | copy-start | bytes 62914564
  261.6 21.9 %copy-start.7 = (f32[128]{0:T(128)S(1)}, f32[128]{0:T(128)}, u32[]{:S(2)}) copy-start(f32[128]{0:T(128)} %param.16) | copy-start | bytes 1540
Sparse Core Ops, SparseCore 0:
  9.7 68.5 all-gather.11
  80.0 109.2 all-gather.5
  191.7 45.0 all-gather.9
  239.0 44.3 all-gather.7
  285.7 63.5 all-gather.13
  363.3 110.3 reduce-scatter.1
where the time goes:
time: 481 us
  waiting for transfers between devices  381 us (79%)
  matrix products  56.1 us (12%)
  other arithmetic  16.3 us (3%)
  local copies, waits for them, and re-layouts  13.8 us (3%)
  between operations  13.6 us (3%)
    all_gather x1, waiting for transfers between devices, project_heads(): piece = lax.all_gather(normed, 'sp', axis=0, tiled=True)  111 us
    reduce_scatter x1, waiting for transfers between devices, body(): lax.psum_scatter(partial_value.astype(jnp.bfloat16), 'sp', scatter_dimens...  111 us
    all_gather x1, waiting for transfers between devices, body(): lax.all_gather(q_weight, 'fsdp', axis=0, tiled=True)  60.9 us
    all_gather x1, waiting for transfers between devices, body(): lax.all_gather(out_weight, 'fsdp', axis=0, tiled=True)  49.7 us
    all_gather x1, waiting for transfers between devices, body(): lax.all_gather(key_matrix, 'fsdp', axis=0, tiled=True)  29 us
    all_gather x1, waiting for transfers between devices, body(): lax.all_gather(value_matrix, 'fsdp', axis=0, tiled=True)  17.1 us
    dot_general x1, matrix products, attend(): jnp.einsum('kgqs,skd->qkgd', probs, value_grid, preferred_element_type=jn...  16.2 us
    dot_general x1, matrix products, body(): lax.dot_general(heads, lax.all_gather(out_weight, 'fsdp', axis=0, tiled=T...  13.8 us
  transfers between devices with their start and end apart: 6, of which 6 were waited for; matrix products, arithmetic and copies ran while one was open for 14% of the time, Pallas kernels for 0%

commit v1 on v0

v1 whole, which is shorter than its diff:
```python
import functools

import jax
import jax.numpy as jnp
import numpy as np
from jax import lax
from jax.experimental import pallas as pl
from jax.experimental.pallas import tpu as pltpu
from jax.sharding import PartitionSpec as P

MESH = pl.DeviceIdType.MESH
WIDTH = 5120
HEAD = 128
GROUP = 5
QC = GROUP * HEAD
WC = QC + 2 * HEAD
SEQ = 1024
ROWS = 128
WR = 320
HR = WR // 2
KC = 1280
NK = WIDTH // KC
OC = 640
NO = WIDTH // OC
N_SEND = 260
F32 = jnp.float32
BF16 = jnp.bfloat16


def rope_tables():
    half = HEAD // 2
    freq = np.float32(1000000.0) ** (-(np.arange(half, dtype=np.float32) * 2.0 / HEAD)).astype(np.float32)
    angle = (np.arange(SEQ, dtype=np.float32)[:, None] * freq[None, :]).astype(np.float64)
    cos = np.cos(angle).astype(np.float32)
    sin = np.sin(angle).astype(np.float32)
    return np.concatenate([cos, cos], 1), np.concatenate([-sin, sin], 1)


def kernel(
    tok_hbm, gain, wq_hbm, wk_hbm, wv_hbm, bq_in, bk_in, bv_in, wo_hbm, cos_hbm, sin_hbm,
    out,
    tok, stage, xb, wb, wob, acc, qb, kb, vb, hb, cosb, sinb, bq, bk, bv,
    prcv, r1, r2, held,
    lsem, ssem, wsem, wosem, wsib, xsem, xsib, swsem, bsem, psem, r1sem, r2sem, fsem,
):
    f = lax.axis_index("fsdp")
    s = lax.axis_index("sp")
    c = f % 2
    zh = (f // 2) % 2
    y = f // 4
    zl = s // 4
    x = s % 4
    z = zh * 2 + zl
    home = c == zl
    away = c != zl
    yp, ym, y2 = (y + 1) % 4, (y + 3) % 4, (y + 2) % 4
    zp, zm, z2 = (z + 1) % 4, (z + 3) % 4, (z + 2) % 4
    xp, xm, x2 = (x + 1) % 4, (x + 3) % 4, (x + 2) % 4

    def dev(y_, z_, x_, c_):
        return ((y_ * 2 + z_ // 2) * 2 + c_, (z_ % 2) * 4 + x_)

    YP, YM = dev(yp, z, x, c), dev(ym, z, x, c)
    ZP, ZM = dev(y, zp, x, c), dev(y, zm, x, c)
    XP, XM = dev(y, z, xp, c), dev(y, z, xm, c)
    SIB = dev(y, z, x, 1 - c)
    SWAP = dev(y, zh * 2 + c, x, zl)

    sends = []

    def send(mk, cond=None):
        k = len(sends)
        mk(ssem.at[k]).start()
        sends.append((cond, mk))

    def wait_sends(lo, hi):
        for cond in (None, home, away):
            group = [(k, sends[k][1]) for k in range(lo, hi) if sends[k][0] is cond]
            if not group:
                continue

            def drain(group=group):
                for k, mk in group:
                    mk(ssem.at[k]).wait_send()

            if cond is None:
                drain()
            else:
                pl.when(cond)(drain)

    def remote(refs, to):
        def mk(sem):
            src, dst, rsem = refs()
            return pltpu.make_async_remote_copy(
                src_ref=src, dst_ref=dst, send_sem=sem, recv_sem=rsem, device_id=to, device_id_type=MESH
            )

        return mk

    def wait_recv(dst, rsem):
        pltpu.make_async_remote_copy(
            src_ref=dst, dst_ref=dst, send_sem=ssem.at[0], recv_sem=rsem, device_id=SIB, device_id_type=MESH
        ).wait_recv()

    pltpu.make_async_copy(tok_hbm, tok, lsem.at[0]).start()
    barrier = pltpu.get_barrier_semaphore()
    for peer in (YP, YM, ZP, ZM, XP, XM, SIB):
        pl.semaphore_signal(barrier, inc=1, device_id=peer, device_id_type=MESH)

    @pl.when(away)
    def _():
        pl.semaphore_signal(barrier, inc=1, device_id=SWAP, device_id_type=MESH)

    pltpu.make_async_copy(cos_hbm, cosb, lsem.at[1]).start()
    pltpu.make_async_copy(sin_hbm, sinb, lsem.at[2]).start()

    def block(y_, z_, i):
        return (y_, z_, i)

    def index_of(b):
        return 4 * b[0] + 2 * (b[1] // 2) + b[2]

    own_f = index_of((y, z, c))
    sib_f = index_of((y, z, 1 - c))

    def own_rows(buf, f_):
        return buf.at[pl.ds(pl.multiple_of(f_ * WR, 32), WR)]

    local_parts = (
        (wq_hbm, wb, 0, QC), (wk_hbm, wb, QC, HEAD), (wv_hbm, wb, QC + HEAD, HEAD), (wo_hbm, wob, 0, QC),
    )

    def part_view(buf, f_, col, n):
        return buf.at[pl.ds(pl.multiple_of(f_ * WR, 32), WR), pl.ds(col, n)]

    @pl.when(home)
    def _():
        for k, (src, buf, col, n) in enumerate(local_parts):
            pltpu.make_async_copy(src, part_view(buf, own_f, col, n), lsem.at[3 + k]).start()
        for k, (src, dst) in enumerate(((bq_in, bq), (bk_in, bk), (bv_in, bv))):
            dst[...] = src[...]

    pltpu.make_async_copy(tok_hbm, tok, lsem.at[0]).wait()
    my_rows = pl.multiple_of(c * (4 * ROWS) + x * ROWS, ROWS)

    def norm_to(dst, base):
        @pl.loop(0, ROWS // 16)
        def _(r):
            r0 = pl.multiple_of(r * 16, 16)
            t = tok[pl.ds(r0, 16), :].astype(F32)
            ms = jnp.mean(t * t, axis=-1, keepdims=True)
            dst[pl.ds(pl.multiple_of(base + r0, 16), 16), :] = (t * lax.rsqrt(ms + 1e-06) * gain[...]).astype(BF16)

    @pl.when(home)
    def _():
        norm_to(xb, my_rows)

    @pl.when(away)
    def _():
        norm_to(stage, 0)

    pl.semaphore_wait(barrier, 7 + (1 - (c == zl).astype(jnp.int32)))

    class Flow:
        def __init__(self, buf, rsem):
            self.buf, self.rsem = buf, rsem

        def refs(self, b, h):
            k = index_of(b)
            v = self.buf.at[pl.ds(pl.multiple_of(k * WR + h * HR, 32), HR)]
            return v, v, self.rsem.at[k, h]

        def fwd(self, b, h, to, cond):
            send(remote(lambda: self.refs(b, h), to), cond)

        def wait(self, b, h):
            _, v, sem = self.refs(b, h)
            wait_recv(v, sem)

        def h0(self):
            for h in (0, 1):
                for to in (YP, YM):
                    self.fwd(block(y, z, 1), h, to, home)
                for to in (ZP, ZM):
                    self.fwd(block(y, z, 0), h, to, home)
            for h in (0, 1):
                for to in (YP, YM):
                    self.fwd(block(y, z, 0), h, to, home)
                for to in (ZP, ZM):
                    self.fwd(block(y, z, 1), h, to, home)

        def relay_y(self, z_, i, cond):
            self.wait(block(ym, z_, i), 0)
            self.fwd(block(ym, z_, i), 0, YP, cond)
            self.wait(block(yp, z_, i), 1)
            self.fwd(block(yp, z_, i), 1, YM, cond)
            self.wait(block(ym, z_, i), 1)
            self.wait(block(yp, z_, i), 0)

        def relay_z(self, y_, i, cond):
            self.wait(block(y_, zm, i), 0)
            self.fwd(block(y_, zm, i), 0, ZP, cond)
            self.wait(block(y_, zp, i), 1)
            self.fwd(block(y_, zp, i), 1, ZM, cond)
            self.wait(block(y_, zm, i), 1)
            self.wait(block(y_, zp, i), 0)

        def both(self, f_, dirs, cond):
            for h in (0, 1):
                for to in dirs:
                    self.fwd(f_, h, to, cond)

        def h1(self):
            self.relay_y(z, 1, home)
            self.both(block(ym, z, 1), (ZP, ZM), home)
            self.both(block(yp, z, 1), (ZP, ZM), home)

        def h2(self):
            self.relay_y(z, 0, home)

        def take(self, f_):
            self.wait(f_, 0)
            self.wait(f_, 1)

        def h3(self):
            self.take(block(y2, z, 1))
            self.both(block(y2, z, 1), (ZP, ZM), home)

        def h4(self):
            self.take(block(y, z2, 0))
            self.both(block(y, z2, 0), (YP, YM), home)
            self.take(block(y, z2, 1))

        def h5(self):
            self.relay_y(z2, 0, home)

        def h6(self):
            self.take(block(ym, z2, 1))
            self.take(block(yp, z2, 1))

        def h7(self):
            self.take(block(y2, z, 0))
            self.take(block(y2, z2, 0))
            self.take(block(y2, z2, 1))

        def n1(self):
            self.relay_z(y, 0, away)
            self.both(block(y, zm, 0), (YP, YM), away)
            self.both(block(y, zp, 0), (YP, YM), away)

        def n2(self):
            self.relay_z(y, 1, away)

        def n3(self):
            self.relay_y(zm, 0, away)
            self.relay_y(zp, 0, away)

        def n4(self):
            self.relay_z(ym, 1, away)
            self.relay_z(yp, 1, away)

        def n5(self):
            self.relay_z(y2, 1, away)

        def n6(self):
            self.take(block(y2, zm, 0))
            self.take(block(y2, zp, 0))

        def step(self, h=(), n=()):
            if h:
                @pl.when(home)
                def _():
                    for name in h:
                        getattr(self, name)()
            if n:
                @pl.when(away)
                def _():
                    for name in n:
                        getattr(self, name)()

    qkv = Flow(wb, wsem)
    wout = Flow(wob, wosem)

    def place(parts, h_flow):
        @pl.when(away)
        def _():
            for k, (src, buf, col, n) in parts:
                send(remote(lambda a=src, b=buf, o=col, m=n, k=k: (a, part_view(b, own_f, o, m), wsib.at[k]), SIB), away)

        @pl.when(home)
        def _():
            for k, (src, buf, col, n) in parts:
                pltpu.make_async_copy(src, part_view(buf, own_f, col, n), lsem.at[3 + k]).wait()
                wait_recv(part_view(buf, sib_f, col, n), wsib.at[k])
            h_flow.h0()

    enum_parts = list(enumerate(local_parts))

    chunk_at = (y, yp, ym, y2)

    def xv(core, x_, kk, r0=0, nr=ROWS):
        return xb.at[
            pl.ds(pl.multiple_of(core * (4 * ROWS) + x_ * ROWS + r0, 16), nr),
            pl.ds(pl.multiple_of(chunk_at[kk] * KC, 128), KC),
        ]

    def x_swap():
        @pl.when(away)
        def _():
            for kk in range(NK):
                send(remote(lambda kk=kk: (
                    stage.at[:, pl.ds(pl.multiple_of(chunk_at[kk] * KC, 128), KC)], xv(1 - c, x, kk), swsem.at[kk]
                ), SWAP), away)
                if kk == 0:
                    for k, (a, b) in enumerate(((bq_in, bq), (bk_in, bk), (bv_in, bv))):
                        send(remote(lambda a=a, b=b, k=k: (a, b, bsem.at[k]), SWAP), away)

    half_rows = ROWS // 2

    def xsend(where, sem, to):
        def refs():
            v = xv(*where)
            return v, v, sem

        send(remote(refs, to))

    def x_own(kk):
        @pl.when(away)
        def _():
            wait_recv(xv(c, x, kk), swsem.at[kk])

        xsend((c, x, kk), xsem.at[kk, 0], XP)
        xsend((c, x, kk), xsem.at[kk, 1], XM)
        xsend((c, x, kk), xsib.at[kk, 0], SIB)

    def x_relay(kk):
        wait_recv(xv(c, xm, kk), xsem.at[kk, 0])
        xsend((c, xm, kk, 0, half_rows), xsem.at[kk, 2], XP)
        wait_recv(xv(c, xp, kk), xsem.at[kk, 1])
        xsend((c, xp, kk, half_rows, half_rows), xsem.at[kk, 3], XM)
        xsend((c, xm, kk), xsib.at[kk, 1], SIB)
        xsend((c, xp, kk), xsib.at[kk, 2], SIB)

    def x_last(kk):
        wait_recv(xv(c, x2, kk, 0, half_rows), xsem.at[kk, 2])
        wait_recv(xv(c, x2, kk, half_rows, half_rows), xsem.at[kk, 3])
        xsend((c, x2, kk), xsib.at[kk, 3], SIB)

    def x_sib(kk):
        for k, x_ in enumerate((x, xm, xp, x2)):
            wait_recv(xv(1 - c, x_, kk), xsib.at[kk, k])

    RB = 256

    def project(kk):
        cols = pl.ds(pl.multiple_of(chunk_at[kk] * KC, 128), KC)

        @pl.loop(0, SEQ // RB)
        def _(r):
            rows = pl.ds(pl.multiple_of(r * RB, RB), RB)
            d = jnp.dot(xb[rows, cols], wb[cols, :], preferred_element_type=F32)
            if kk == 0:
                acc[rows, :] = d
            else:
                acc[rows, :] += d

    x_swap()
    place(enum_parts[:3], qkv)
    x_own(0)
    x_own(1)
    qkv.step(h=("h1",), n=("n1",))
    x_relay(0)
    qkv.step(h=("h2",), n=("n2",))
    x_own(2)
    x_last(0)
    qkv.step(h=("h3", "h4"))
    x_relay(1)
    x_own(3)
    x_sib(0)
    project(0)
    x_last(1)
    qkv.step(h=("h5",), n=("n3", "n4"))
    x_relay(2)
    x_sib(1)
    x_last(2)
    x_sib(2)
    qkv.step(h=("h6",), n=("n5",))
    place(enum_parts[3:], wout)
    project(1)
    x_relay(3)
    project(2)
    x_last(3)
    qkv.step(h=("h7",), n=("n6",))
    x_sib(3)
    project(3)
    wout.step(h=("h1",), n=("n1",))

    pltpu.make_async_copy(cos_hbm, cosb, lsem.at[1]).wait()
    pltpu.make_async_copy(sin_hbm, sinb, lsem.at[2]).wait()

    @pl.when(away)
    def _():
        for k, b in enumerate((bq, bk, bv)):
            wait_recv(b, bsem.at[k])

    @pl.loop(0, SEQ // 128)
    def _(r):
        rows = pl.ds(pl.multiple_of(r * 128, 128), 128)
        cs, sn = cosb[rows, :], sinb[rows, :]
        for h in range(GROUP + 1):
            col = slice(h * HEAD, (h + 1) * HEAD)
            bias = bq[:, col] if h < GROUP else bk[...]
            t = acc[rows, col] + bias
            t = (t * cs + pltpu.roll(t, HEAD // 2, 1) * sn).astype(BF16)
            if h < GROUP:
                qb[rows, col] = t
            else:
                kb[rows, :] = t
        vb[rows, :] = (acc[rows, QC + HEAD :] + bv[...]).astype(BF16)

    scale = 1.0 / float(np.sqrt(np.float32(HEAD)))
    QB = 256

    def attend(i):
        n = (i + 1) * QB

        @pl.loop(0, GROUP)
        def _(h):
            col = pl.ds(pl.multiple_of(h * HEAD, HEAD), HEAD)
            q = qb[i * QB : n, col]
            sc = lax.dot_general(q, kb[:n, :], (((1,), (1,)), ((), ())), preferred_element_type=F32) * scale
            qi = lax.broadcasted_iota(jnp.int32, (QB, n), 0) + i * QB
            ki = lax.broadcasted_iota(jnp.int32, (QB, n), 1)
            sc = jnp.where(qi >= ki, sc, -1e30)
            w = jnp.exp(sc - jnp.max(sc, axis=-1, keepdims=True))
            tot = jnp.sum(w, axis=-1, keepdims=True)
            o = jnp.dot(w.astype(BF16), vb[:n, :], preferred_element_type=F32)
            hb[i * QB : n, col] = (o / tot).astype(BF16)

    attend(0)
    wout.step(h=("h2",), n=("n2",))
    attend(1)
    wout.step(h=("h3", "h4"))
    attend(2)
    attend(3)

    n_phase1 = len(sends)
    wait_sends(0, n_phase1)

    def st(r0, nr, j):
        return xb.at[pl.ds(r0, nr), pl.ds(j * OC, OC)]

    def out_at(j):
        ky, k2 = chunk_at[j // 2], j % 2
        return (ky * 2 + k2) * OC

    def terms(j):
        wrow = pl.ds(pl.multiple_of(out_at(j), 128), OC)

        def dot(row):
            return lax.dot_general(
                hb[pl.ds(pl.multiple_of(row, 128), 256), :], wob[wrow, :], (((1,), (1,)), ((), ())),
                preferred_element_type=F32,
            )

        @pl.loop(0, 2)
        def _(r):
            xb[pl.ds(pl.multiple_of(r * 256, 256), 256), pl.ds(j * OC, OC)] = dot((1 - c) * 512 + r * 256).astype(BF16)

        send(remote(lambda: (st(0, 512, j), prcv.at[j], psem.at[j]), SIB))

        @pl.loop(0, 2)
        def _(r):
            acc[pl.ds(pl.multiple_of((j % 2) * 512 + r * 256, 256), 256), pl.ds(0, OC)] = dot(c * 512 + r * 256)

    def pair(j):
        wait_recv(prcv.at[j], psem.at[j])
        oc = pl.ds(j * OC, OC)

        def total(x_, h):
            r0 = x_ * ROWS + h * half_rows
            mine = acc[pl.ds(pl.multiple_of((j % 2) * 512 + r0, 64), half_rows), pl.ds(0, OC)]
            return mine + prcv[j, pl.ds(pl.multiple_of(r0, 64), half_rows), :].astype(F32)

        for h in (0, 1):
            xb[512 + h * 64 : 576 + h * 64, oc] = total(x2, h).astype(BF16)
        send(remote(lambda: (st(512, 64, j), r1.at[j, 0], r1sem.at[j, 0]), XP))
        send(remote(lambda: (st(576, 64, j), r1.at[j, 1], r1sem.at[j, 1]), XM))
        xb[704:768, oc] = total(xp, 1).astype(BF16)
        xb[768:832, oc] = total(xm, 0).astype(BF16)
        send(remote(lambda: (st(704, 64, j), r2.at[j, 1], r2sem.at[j, 1]), XP))
        send(remote(lambda: (st(768, 64, j), r2.at[j, 2], r2sem.at[j, 2]), XM))
        held[j, 0] = total(xp, 0)
        held[j, 1] = total(xm, 1)
        held[j, 2] = total(x, 0)
        held[j, 3] = total(x, 1)

    def relay(j):
        oc = pl.ds(j * OC, OC)
        wait_recv(r1.at[j, 0], r1sem.at[j, 0])
        xb[640:704, oc] = (held[j, 0] + r1[j, 0].astype(F32)).astype(BF16)
        send(remote(lambda: (st(640, 64, j), r2.at[j, 0], r2sem.at[j, 0]), XP))
        wait_recv(r1.at[j, 1], r1sem.at[j, 1])
        xb[832:896, oc] = (held[j, 1] + r1[j, 1].astype(F32)).astype(BF16)
        send(remote(lambda: (st(832, 64, j), r2.at[j, 3], r2sem.at[j, 3]), XM))

    def out_cols(j):
        return pl.ds(pl.multiple_of(out_at(j), 128), OC)

    def final(j):
        oc = pl.ds(j * OC, OC)
        for k in range(4):
            wait_recv(r2.at[j, k], r2sem.at[j, k])

        def whole(h):
            return (held[j, 2 + h] + r2[j, h].astype(F32) + r2[j, 2 + h].astype(F32)).astype(BF16)

        @pl.when(home)
        def _():
            for h in (0, 1):
                out[h * 64 : h * 64 + 64, out_cols(j)] = whole(h)

        @pl.when(away)
        def _():
            for h in (0, 1):
                xb[896 + h * 64 : 960 + h * 64, oc] = whole(h)
            send(remote(lambda: (st(896, 128, j), out.at[:, out_cols(j)], fsem.at[j]), SWAP), away)

    for it in range(NO + 3):
        if it == 2:
            wout.step(h=("h5",), n=("n3", "n4"))
            wout.step(h=("h6",))
        if it == 4:
            wout.step(n=("n5",))
        if it == 6:
            wout.step(h=("h7",), n=("n6",))
        if it < NO:
            terms(it)
        if 0 <= it - 1 < NO:
            pair(it - 1)
        if 0 <= it - 2 < NO:
            relay(it - 2)
        if 0 <= it - 3 < NO:
            final(it - 3)

    @pl.when(away)
    def _():
        for j in range(NO):
            wait_recv(out.at[:, out_cols(j)], fsem.at[j])

    wait_sends(n_phase1, len(sends))
    assert len(sends) <= N_SEND, len(sends)


def body(tokens, gain, wq, wk, wv, bq, bk, bv, wo):
    cos, sin = rope_tables()
    any_, vm = pl.BlockSpec(memory_space=pl.ANY), pl.BlockSpec(memory_space=pltpu.VMEM)
    dma = lambda *n: pltpu.SemaphoreType.DMA(n)
    return pl.pallas_call(
        kernel,
        out_shape=jax.ShapeDtypeStruct((ROWS, WIDTH), BF16),
        in_specs=[any_, vm, any_, any_, any_, vm, vm, vm, any_, any_, any_],
        out_specs=vm,
        scratch_shapes=[
            pltpu.VMEM((ROWS, WIDTH), BF16),
            pltpu.VMEM((ROWS, WIDTH), BF16),
            pltpu.VMEM((SEQ, WIDTH), BF16),
            pltpu.VMEM((WIDTH, WC), BF16),
            pltpu.VMEM((WIDTH, QC), BF16),
            pltpu.VMEM((SEQ, WC), F32),
            pltpu.VMEM((SEQ, QC), BF16),
            pltpu.VMEM((SEQ, HEAD), BF16),
            pltpu.VMEM((SEQ, HEAD), BF16),
            pltpu.VMEM((SEQ, QC), BF16),
            pltpu.VMEM((SEQ, HEAD), F32),
            pltpu.VMEM((SEQ, HEAD), F32),
            pltpu.VMEM((1, QC), F32),
            pltpu.VMEM((1, HEAD), F32),
            pltpu.VMEM((1, HEAD), F32),
            pltpu.VMEM((NO, 512, OC), BF16),
            pltpu.VMEM((NO, 2, 64, OC), BF16),
            pltpu.VMEM((NO, 4, 64, OC), BF16),
            pltpu.VMEM((NO, 4, 64, OC), F32),
            dma(8), dma(N_SEND), dma(16, 2), dma(16, 2), dma(4), dma(NK, 4), dma(NK, 4), dma(NK), dma(3),
            dma(NO), dma(NO, 2), dma(NO, 4), dma(NO),
        ],
        compiler_params=pltpu.CompilerParams(
            collective_id=0, has_side_effects=True, vmem_limit_bytes=67043328
        ),
    )(
        tokens, gain.reshape(1, -1), wq, wk, wv, bq.reshape(1, -1), bk.reshape(1, -1), bv.reshape(1, -1), wo,
        jnp.asarray(cos), jnp.asarray(sin),
    )


def solution(mesh):
    placed = (
        P(("fsdp", "sp"), None), P(), P("fsdp", "sp"), P("fsdp", "sp"), P("fsdp", "sp"),
        P("sp"), P("sp"), P("sp"), P("fsdp", "sp"),
    )
    return jax.shard_map(
        body, mesh=mesh, in_specs=placed, out_specs=P(("fsdp", "sp"), None), check_vma=False
    )
```

time: 481 us -> 162 us (0.34)
  waiting for transfers between devices: 381 us -> 0 us
  Pallas kernels: 0 us -> 158 us
  matrix products: 56.1 us -> 0 us
  other arithmetic: 16.3 us -> 0 us
  between operations: 13.6 us -> 0.01 us
  local copies, waits for them, and re-layouts: 13.8 us -> 3.72 us
    all_gather x5 -> x0, waiting for transfers between devices: 268 us -> none  [the longest x1 111 us: project_heads(): piece = lax.all_gather(normed, 'sp', axis=0, tiled=True)]
    pallas_call x0 -> x1, Pallas kernels: none -> 158 us  [body(): pl.pallas_call(kernel, out_shape=jax.ShapeDtypeStruct((ROWS, WIDTH), BF16...]
    reduce_scatter x1 -> x0, waiting for transfers between devices: 111 us -> none  [body(): lax.psum_scatter(partial_value.astype(jnp.bfloat16), 'sp', scatter_dimens...]
    dot_general x5 -> x0, matrix products: 56.1 us -> none  [the longest x1 16.2 us: attend(): jnp.einsum('kgqs,skd->qkgd', probs, value_grid, preferred_element_type=jn...]
    unnamed x18 -> x1, local copies, waits for them, and re-layouts: 11.9 us -> 2.46 us
    reduce_sum x2 -> x0, other arithmetic: 6.41 us -> none  [the longest x1 4.76 us: attend(): totals = jnp.sum(weights, axis=-1, keepdims=True)]
  transfers between devices with their start and end apart: 6 -> 0, of which waited for: 6 -> 0; matrix products, arithmetic and copies ran while one was open for 14% -> 0% of each run, Pallas kernels for 0% -> 0%
where the time goes in v1:
time: 162 us
  Pallas kernels  158 us (98%)
  local copies, waits for them, and re-layouts  3.72 us (2%)
    pallas_call x1, Pallas kernels, body(): pl.pallas_call(kernel, out_shape=jax.ShapeDtypeStruct((ROWS, WIDTH), BF16...  158 us

profile of v1, /device:TPU:1, one launch (start us, length us, event | category | flops | bytes accessed | tf_op | source)
XLA Modules:
  0.0 162.2 jit_solution(3568626022902207727)
XLA Ops:
  0.0 1.3 reshape.13.bq_in
  1.3 158.5 %shard_map.109 = bf16[128,5120]{1,0:T(8,128)(2,1)} custom-call(bf16[128,5120]{1,0:T(8,128)(2,1)} %tok_hbm.1, f32[1,5120]{1,0:T(1,128)} %bitcast.3, bf16[320,640]{1,0:T(8,128)(2,1)} %wq_hbm.1, bf16[320,128]{1,0:T(8,128)(2,1)} %wk_hbm.1, bf16[320,128]{1,0:T(8,128)(2,1)} %wv_hbm.1, f32[1,640]{1,0:T(1,128)} %reshape.13.bq_in, f32[1,128]{1,0:T(1,128)} %bitcast.4, ...), custom_call_target="tpu_custom_call" | custom-call | tf_op jit(solution)/shard_map/pallas_call | solution.py:559
  159.8 2.5 %copy.13 = bf16[128,5120]{1,0:T(8,128)(2,1)} copy(bf16[128,5120]{1,0:T(8,128)(2,1)} %shard_map.109) | data formatting | bytes 2621440

commit v2 on v1

v2 whole, which is shorter than its diff:
```python
import functools

import jax
import jax.numpy as jnp
import numpy as np
from jax import lax
from jax.experimental import pallas as pl
from jax.experimental.pallas import tpu as pltpu
from jax.sharding import PartitionSpec as P

MESH = pl.DeviceIdType.MESH
WIDTH = 5120
HEAD = 128
GROUP = 5
QC = GROUP * HEAD
WC = QC + 2 * HEAD
SEQ = 1024
ROWS = 128
WR = 320
HR = WR // 2
KC = 1280
NK = WIDTH // KC
OC = 640
NO = WIDTH // OC
N_SEND = 300
F32 = jnp.float32
BF16 = jnp.bfloat16
LATE_Q, OUTER_Q = 0, (0, 2)
LATE_O, OUTER_O = 1, (0, 2, 3)
SCHEDULE = (
    "qo", "xw", "xo0", "qn1", "xr0", "xo1", "xo2", "qs", "qh1", "qh3", "qh2", "qn2", "xl0", "wo", "xo3", "xr1",
    "qh4", "xr2", "qn4a", "xl1", "qh5", "xl2", "xs0", "xs1", "ws", "xr3", "qh4b", "p00", "qn4b", "qn3a", "wh1", "xs2",
    "p01", "qn3b", "p20", "qn5", "qh7b", "xl3", "p10", "qh7a", "qh6", "p11", "p21", "qn6b", "qn6a", "xs3", "p30", "wn1",
    "qh8", "p31", "e", "a302", "wn2", "a325", "a105", "a005", "d", "a202", "wh4b", "t00", "a225", "wn4a", "t10", "g10",
    "g00", "r00", "wn4b", "wn3a", "wh3", "r10", "wh2", "wh4", "t12", "g12", "t14", "g14", "f00", "t02", "r12", "g02",
    "t11", "t04", "wn5", "g11", "wn6a", "g04", "wh7a", "t16", "t01", "g01", "wh6", "wn3b", "g16", "t06", "f10", "g06",
    "wh5", "t03", "t13", "r01", "r04", "r06", "g03", "wh7b", "t05", "r02", "wh8", "r11", "r14", "r16", "g05", "g13",
    "t15", "wn6b", "t07", "r13", "f11", "g15", "t17", "f12", "r03", "f06", "g07", "f04", "f01", "f13", "f02", "r05",
    "f16", "g17", "r07", "f03", "r15", "f05", "r17", "f07", "f14", "f15", "f17",
)


def rope_tables():
    half = HEAD // 2
    freq = np.float32(1000000.0) ** (-(np.arange(half, dtype=np.float32) * 2.0 / HEAD)).astype(np.float32)
    angle = (np.arange(SEQ, dtype=np.float32)[:, None] * freq[None, :]).astype(np.float64)
    cos = np.cos(angle).astype(np.float32)
    sin = np.sin(angle).astype(np.float32)
    return np.concatenate([cos, sin], 1)


def kernel(
    tok_hbm, gain, wq_hbm, wk_hbm, wv_hbm, bq_in, bk_in, bv_in, wo_hbm, trig_hbm,
    out,
    tok, stage, xb, wb, wob, acc, qb, kb, vb, hb, trig, bq, bk, bv,
    prcv, r1, r2, held,
    lsem, ssem, wsem, wosem, wsib, xsem, xsib, swsem, bsem, psem, r1sem, r2sem, fsem,
):
    f = lax.axis_index("fsdp")
    s = lax.axis_index("sp")
    c = f % 2
    zh = (f // 2) % 2
    y = f // 4
    zl = s // 4
    x = s % 4
    z = zh * 2 + zl
    home = c == zl
    away = c != zl
    cores = (c == 0, c == 1)
    aways = ((c == 0) & away, (c == 1) & away)
    yp, ym, y2 = (y + 1) % 4, (y + 3) % 4, (y + 2) % 4
    zp, zm, z2 = (z + 1) % 4, (z + 3) % 4, (z + 2) % 4
    xp, xm, x2 = (x + 1) % 4, (x + 3) % 4, (x + 2) % 4

    def dev(y_, z_, x_, c_):
        return ((y_ * 2 + z_ // 2) * 2 + c_, (z_ % 2) * 4 + x_)

    YP, YM = dev(yp, z, x, c), dev(ym, z, x, c)
    ZP, ZM = dev(y, zp, x, c), dev(y, zm, x, c)
    XP, XM = dev(y, z, xp, c), dev(y, z, xm, c)
    SIB = dev(y, z, x, 1 - c)
    SWAP = dev(y, zh * 2 + c, x, zl)

    sends, token = [], [None]

    def send(mk, cond=None):
        k = len(sends)
        mk(ssem.at[k]).start()
        sends.append((cond, mk, token[0]))

    def wait_sends(of_tokens):
        for cond in (None, home, away, *cores, *aways):
            group = [(k, e[1]) for k, e in enumerate(sends) if e[0] is cond and (e[2] == "x") == of_tokens]
            if not group:
                continue

            def drain(group=group):
                for k, mk in group:
                    mk(ssem.at[k]).wait_send()

            if cond is None:
                drain()
            else:
                pl.when(cond)(drain)

    def remote(refs, to):
        def mk(sem):
            src, dst, rsem = refs()
            return pltpu.make_async_remote_copy(
                src_ref=src, dst_ref=dst, send_sem=sem, recv_sem=rsem, device_id=to, device_id_type=MESH
            )

        return mk

    def wait_recv(dst, rsem):
        pltpu.make_async_remote_copy(
            src_ref=dst, dst_ref=dst, send_sem=ssem.at[0], recv_sem=rsem, device_id=SIB, device_id_type=MESH
        ).wait_recv()

    pltpu.make_async_copy(tok_hbm, tok, lsem.at[0]).start()
    barrier = pltpu.get_barrier_semaphore()
    for peer in (YP, YM, ZP, ZM, XP, XM, SIB):
        pl.semaphore_signal(barrier, inc=1, device_id=peer, device_id_type=MESH)

    @pl.when(away)
    def _():
        pl.semaphore_signal(barrier, inc=1, device_id=SWAP, device_id_type=MESH)

    pltpu.make_async_copy(trig_hbm, trig, lsem.at[1]).start()

    def block(y_, z_, i):
        return (y_, z_, i)

    def index_of(b):
        return 4 * b[0] + 2 * (b[1] // 2) + b[2]

    own_f = index_of((y, z, c))
    sib_f = index_of((y, z, 1 - c))

    def own_rows(buf, f_):
        return buf.at[pl.ds(pl.multiple_of(f_ * WR, 32), WR)]

    local_parts = (
        (wq_hbm, wb, 0, QC), (wk_hbm, wb, QC, HEAD), (wv_hbm, wb, QC + HEAD, HEAD), (wo_hbm, wob, 0, QC),
    )

    def part_view(buf, f_, col, n):
        return buf.at[pl.ds(pl.multiple_of(f_ * WR, 32), WR), pl.ds(col, n)]

    @pl.when(home)
    def _():
        for k, (src, buf, col, n) in enumerate(local_parts):
            pltpu.make_async_copy(src, part_view(buf, own_f, col, n), lsem.at[3 + k]).start()
        for k, (src, dst) in enumerate(((bq_in, bq), (bk_in, bk), (bv_in, bv))):
            dst[...] = src[...]

    pltpu.make_async_copy(tok_hbm, tok, lsem.at[0]).wait()
    my_rows = pl.multiple_of(c * (4 * ROWS) + x * ROWS, ROWS)

    def norm_to(dst, base):
        @pl.loop(0, ROWS // 16)
        def _(r):
            r0 = pl.multiple_of(r * 16, 16)
            t = tok[pl.ds(r0, 16), :].astype(F32)
            ms = jnp.mean(t * t, axis=-1, keepdims=True)
            dst[pl.ds(pl.multiple_of(base + r0, 16), 16), :] = (t * lax.rsqrt(ms + 1e-06) * gain[...]).astype(BF16)

    @pl.when(home)
    def _():
        norm_to(xb, my_rows)

    @pl.when(away)
    def _():
        norm_to(stage, 0)

    pl.semaphore_wait(barrier, 7 + (c + zl) % 2)

    zq, zn = z + 1 - 2 * zl, (z + 3 + 2 * zl) % 4
    ZN = dev(y, zn, x, c)

    class Flow:
        def __init__(self, buf, rsem, late, outer):
            self.buf, self.rsem = buf, rsem
            self.own = [(0, 0), (0, 1)]
            self.sib = [(1, 0), (1, 1)]
            self.zfirst = self.sib + self.own[2 - late :]
            self.yfirst = self.own[: 2 - late]
            self.outer = outer

        def refs(self, y_, z_, u):
            k = 4 * y_ + 2 * (z_ // 2) + (c + u[0]) % 2
            v = self.buf.at[pl.ds(pl.multiple_of(k * WR + u[1] * HR, 32), HR)]
            return v, v, self.rsem.at[k, u[1]]

        def fwd(self, y_, z_, u, to, cond):
            send(remote(lambda: self.refs(y_, z_, u), to), cond)

        def wait(self, y_, z_, units):
            for u in units:
                _, v, sem = self.refs(y_, z_, u)
                wait_recv(v, sem)

        def spread(self, y_, z_, units, dirs, cond):
            for u in units:
                for to in dirs:
                    self.fwd(y_, z_, u, to, cond)

        def relay_y(self, z_, units, flip, cond):
            for n, u in enumerate(units):
                for y_, to, turn in ((ym, YP, 0), (yp, YM, 1)):
                    self.wait(y_, z_, [u])
                    if (n + flip) % 2 == turn:
                        self.fwd(y_, z_, u, to, cond)

        def relay_z(self, y_, units, row, cond):
            for n, u in enumerate(units):
                if row in self.outer:
                    self.wait(y_, zq, [u])
                    self.fwd(y_, zq, u, ZN, cond)
                    self.wait(y_, zn, [u])
                    continue
                for z_, to, turn in ((zm, ZP, 0), (zp, ZM, 1)):
                    self.wait(y_, z_, [u])
                    if n % 2 == turn:
                        self.fwd(y_, z_, u, to, cond)

        def h0(self):
            for u in self.own:
                self.spread(y, z, [u], (YP, YM, ZP, ZM), home)

        def h0s(self):
            for u in self.sib:
                self.spread(y, z, [u], (ZP, ZM, YP, YM), home)

        def h1(self):
            self.relay_y(z, self.yfirst, 0, home)
            self.spread(ym, z, self.yfirst, (ZP, ZM), home)
            self.spread(yp, z, self.yfirst, (ZP, ZM), home)

        def h2(self):
            self.relay_y(z, self.zfirst, len(self.yfirst), home)

        def h3(self):
            self.wait(y2, z, self.yfirst)
            self.spread(y2, z, self.yfirst, (ZP, ZM), home)

        def h4(self):
            for u in self.zfirst[::-1]:
                self.wait(y, z2, [u])
                self.spread(y, z2, [u], (YP, YM), home)

        def h4b(self):
            self.wait(y, z2, self.yfirst)

        def h5(self):
            self.relay_y(z2, self.zfirst[::-1], 0, home)

        def h6(self):
            self.wait(ym, z2, self.yfirst)
            self.wait(yp, z2, self.yfirst)

        def h7a(self):
            self.wait(y2, z, self.zfirst)

        def h7b(self):
            self.wait(y2, z2, self.zfirst)

        def h8(self):
            self.wait(y2, z2, self.yfirst)

        def n1(self):
            self.relay_z(y, self.own, 0, away)
            u = self.own[2 - len(self.zfirst) + 2 :]
            for v in u:
                for z_ in (zm, zp):
                    self.spread(y, z_, [v], (YP, YM), away)

        def n2(self):
            self.relay_z(y, self.sib, 1, away)
            for v in self.sib:
                for z_ in (zm, zp):
                    self.spread(y, z_, [v], (YP, YM), away)

        def n3a(self):
            self.relay_y(zq, self.order_n(), 0, away)

        def n3b(self):
            self.relay_y(zn, self.order_n(), 1, away)

        def order_n(self):
            return [u for u in self.zfirst if u[0] == 0] + self.sib

        def n4a(self):
            self.relay_z(ym, self.yfirst, 2, away)

        def n4b(self):
            self.relay_z(yp, self.yfirst, 3, away)

        def n5(self):
            self.relay_z(y2, self.yfirst, 4, away)

        def n6a(self):
            self.wait(y2, zq, self.zfirst)

        def n6b(self):
            self.wait(y2, zn, self.zfirst)

        def step(self, name):
            @pl.when(home if name[0] == "h" else away)
            def _():
                getattr(self, name)()

    qkv = Flow(wb, wsem, LATE_Q, OUTER_Q)
    wout = Flow(wob, wosem, LATE_O, OUTER_O)

    def place_own(parts, flow):
        @pl.when(away)
        def _():
            for k, (src, buf, col, n) in parts:
                send(remote(lambda a=src, b=buf, o=col, m=n, k=k: (a, part_view(b, own_f, o, m), wsib.at[k]), SIB), away)

        @pl.when(home)
        def _():
            for k, (src, buf, col, n) in parts:
                pltpu.make_async_copy(src, part_view(buf, own_f, col, n), lsem.at[3 + k]).wait()
            flow.h0()

    def place_sib(parts, flow):
        @pl.when(home)
        def _():
            for k, (src, buf, col, n) in parts:
                wait_recv(part_view(buf, sib_f, col, n), wsib.at[k])
            flow.h0s()

    parts_of = {"q": list(enumerate(local_parts))[:3], "w": list(enumerate(local_parts))[3:]}

    chunk_at = (y, yp, ym, y2)

    def xv(core, x_, kk, r0=0, nr=ROWS):
        return xb.at[
            pl.ds(pl.multiple_of(core * (4 * ROWS) + x_ * ROWS + r0, 16), nr),
            pl.ds(pl.multiple_of(chunk_at[kk] * KC, 128), KC),
        ]

    def x_swap():
        @pl.when(away)
        def _():
            for kk in range(NK):
                send(remote(lambda kk=kk: (
                    stage.at[:, pl.ds(pl.multiple_of(chunk_at[kk] * KC, 128), KC)], xv(1 - c, x, kk), swsem.at[kk]
                ), SWAP), away)
                if kk == 0:
                    for k, (a, b) in enumerate(((bq_in, bq), (bk_in, bk), (bv_in, bv))):
                        send(remote(lambda a=a, b=b, k=k: (a, b, bsem.at[k]), SWAP), away)

    half_rows = ROWS // 2

    def xsend(where, sem, to):
        def refs():
            v = xv(*where)
            return v, v, sem

        send(remote(refs, to))

    def x_own(kk):
        @pl.when(away)
        def _():
            wait_recv(xv(c, x, kk), swsem.at[kk])

        xsend((c, x, kk), xsem.at[kk, 0], XP)
        xsend((c, x, kk), xsem.at[kk, 1], XM)
        xsend((c, x, kk), xsib.at[kk, 0], SIB)

    def x_relay(kk):
        wait_recv(xv(c, xm, kk), xsem.at[kk, 0])
        xsend((c, xm, kk, 0, half_rows), xsem.at[kk, 2], XP)
        wait_recv(xv(c, xp, kk), xsem.at[kk, 1])
        xsend((c, xp, kk, half_rows, half_rows), xsem.at[kk, 3], XM)
        xsend((c, xm, kk), xsib.at[kk, 1], SIB)
        xsend((c, xp, kk), xsib.at[kk, 2], SIB)

    def x_last(kk):
        wait_recv(xv(c, x2, kk, 0, half_rows), xsem.at[kk, 2])
        wait_recv(xv(c, x2, kk, half_rows, half_rows), xsem.at[kk, 3])
        xsend((c, x2, kk), xsib.at[kk, 3], SIB)

    def x_sib(kk):
        for k, x_ in enumerate((x, xm, xp, x2)):
            wait_recv(xv(1 - c, x_, kk), xsib.at[kk, k])

    RB = 256

    def feature_block(kk, side):
        return (chunk_at[kk] * 2 + (zh + side) % 2) * OC

    started = []

    def project(kk, side):
        cols = pl.ds(pl.multiple_of(feature_block(kk, side), 128), OC)
        first = not started
        started.append(kk)

        @pl.loop(0, SEQ // RB)
        def _(r):
            rows = pl.ds(pl.multiple_of(r * RB, RB), RB)
            d = jnp.dot(xb[rows, cols], wb[cols, :], preferred_element_type=F32)
            if first:
                acc[rows, :] = d
            else:
                acc[rows, :] += d

    def rope():
        pltpu.make_async_copy(trig_hbm, trig, lsem.at[1]).wait()

        @pl.when(away)
        def _():
            for k, b in enumerate((bq, bk, bv)):
                wait_recv(b, bsem.at[k])

        @pl.loop(0, SEQ // 128)
        def _(r):
            rows = pl.ds(pl.multiple_of(r * 128, 128), 128)
            here = trig[rows, :]
            other = pltpu.roll(here, HEAD // 2, 1)
            low = lax.broadcasted_iota(jnp.int32, (128, HEAD), 1) < HEAD // 2
            cs, sn = jnp.where(low, here, other), jnp.where(low, -other, here)
            for h in range(GROUP + 1):
                col = slice(h * HEAD, (h + 1) * HEAD)
                bias = bq[col][None, :] if h < GROUP else bk[...]
                t = acc[rows, col] + bias
                t = (t * cs + pltpu.roll(t, HEAD // 2, 1) * sn).astype(BF16)
                if h < GROUP:
                    qb[rows, col] = t
                else:
                    kb[rows, :] = t
            vb[rows, :] = (acc[rows, QC + HEAD :] + bv[...]).astype(BF16)

    scale = float(np.log2(np.e)) / float(np.sqrt(HEAD))
    QB = 256

    def attend(i, lo, hi):
        n = (i + 1) * QB

        @pl.loop(lo, hi, unroll=hi - lo)
        def _(h):
            col = pl.ds(pl.multiple_of(h * HEAD, HEAD), HEAD)
            q = qb[i * QB : n, col]
            near, far = slice(i * QB, n), slice(0, i * QB)

            def score(part):
                return lax.dot_general(q, kb[part, :], (((1,), (1,)), ((), ())), preferred_element_type=F32)

            qi = lax.broadcasted_iota(jnp.int32, (QB, QB), 0)
            ki = lax.broadcasted_iota(jnp.int32, (QB, QB), 1)
            parts = [(near, jnp.where(qi >= ki, score(near), -1e30))] + ([(far, score(far))] if i else [])
            top = functools.reduce(jnp.maximum, [jnp.max(sc, axis=-1, keepdims=True) for _, sc in parts])
            tot, o = 0.0, 0.0
            for part, sc in parts:
                w = jnp.exp2((sc - top) * scale)
                tot += jnp.sum(w, axis=-1, keepdims=True)
                o += jnp.dot(w.astype(BF16), vb[part, :], preferred_element_type=F32)
            hb[near, col] = (o / tot).astype(BF16)

    def st(r0, nr, j):
        return xb.at[pl.ds(r0, nr), pl.ds(j * OC, OC)]

    def out_at(j):
        return feature_block(j // 2, j % 2)

    def terms(st_, j):
        wrow = pl.ds(pl.multiple_of(out_at(j), 128), OC)

        @pl.loop(0, 2)
        def _(r):
            rows = pl.ds(pl.multiple_of(st_ * 512 + r * 256, 256), 256)
            acc[rows, pl.ds(0, OC)] = lax.dot_general(
                hb[rows, :], wob[wrow, :], (((1,), (1,)), ((), ())), preferred_element_type=F32
            )

        @pl.when(c != st_)
        def _():
            @pl.loop(0, 8)
            def _(r):
                r0 = pl.multiple_of(r * 64, 64)
                xb[pl.ds(r0, 64), pl.ds(j * OC, OC)] = acc[pl.ds(st_ * 512 + r0, 64), pl.ds(0, OC)].astype(BF16)

            send(remote(lambda: (st(0, 512, j), prcv.at[j], psem.at[j]), SIB), cores[1 - st_])

    def pair(st_, j, mine_):
        wait_recv(prcv.at[j], psem.at[j])
        oc = pl.ds(j * OC, OC)

        def total(x_, h):
            r0 = x_ * ROWS + h * half_rows
            mine = acc[pl.ds(pl.multiple_of(st_ * 512 + r0, 64), half_rows), pl.ds(0, OC)]
            return mine + prcv[j, pl.ds(pl.multiple_of(r0, 64), half_rows), :].astype(F32)

        for h in (0, 1):
            xb[512 + h * 64 : 576 + h * 64, oc] = total(x2, h).astype(BF16)
        send(remote(lambda: (st(512, 64, j), r1.at[j, 0], r1sem.at[j, 0]), XP), mine_)
        send(remote(lambda: (st(576, 64, j), r1.at[j, 1], r1sem.at[j, 1]), XM), mine_)
        xb[704:768, oc] = total(xp, 1).astype(BF16)
        xb[768:832, oc] = total(xm, 0).astype(BF16)
        send(remote(lambda: (st(704, 64, j), r2.at[j, 1], r2sem.at[j, 1]), XP), mine_)
        send(remote(lambda: (st(768, 64, j), r2.at[j, 2], r2sem.at[j, 2]), XM), mine_)
        held[j, 0] = total(xp, 0)
        held[j, 1] = total(xm, 1)
        held[j, 2] = total(x, 0)
        held[j, 3] = total(x, 1)

    def relay(st_, j, mine_):
        oc = pl.ds(j * OC, OC)
        wait_recv(r1.at[j, 0], r1sem.at[j, 0])
        xb[640:704, oc] = (held[j, 0] + r1[j, 0].astype(F32)).astype(BF16)
        send(remote(lambda: (st(640, 64, j), r2.at[j, 0], r2sem.at[j, 0]), XP), mine_)
        wait_recv(r1.at[j, 1], r1sem.at[j, 1])
        xb[832:896, oc] = (held[j, 1] + r1[j, 1].astype(F32)).astype(BF16)
        send(remote(lambda: (st(832, 64, j), r2.at[j, 3], r2sem.at[j, 3]), XM), mine_)

    def out_cols(j):
        return pl.ds(pl.multiple_of(out_at(j), 128), OC)

    def final(st_, j, mine_):
        oc = pl.ds(j * OC, OC)
        for k in range(4):
            wait_recv(r2.at[j, k], r2sem.at[j, k])

        def whole(h):
            return (held[j, 2 + h] + r2[j, h].astype(F32) + r2[j, 2 + h].astype(F32)).astype(BF16)

        @pl.when(home)
        def _():
            for h in (0, 1):
                out[h * 64 : h * 64 + 64, out_cols(j)] = whole(h)

        @pl.when(away)
        def _():
            for h in (0, 1):
                xb[896 + h * 64 : 960 + h * 64, oc] = whole(h)
            send(remote(lambda: (st(896, 128, j), out.at[:, out_cols(j)], fsem.at[j]), SWAP), aways[st_])

    def ring(fn, st_, j):
        pl.when(cores[st_])(lambda: fn(st_, j, cores[st_]))

    for tok_ in SCHEDULE:
        kind, arg = tok_[0], tok_[1:]
        token[0] = kind
        if kind == "x":
            {"w": x_swap, "o": x_own, "r": x_relay, "l": x_last, "s": x_sib}[arg[0]](*map(int, arg[1:]))
        elif kind in "qw" and arg == "o":
            place_own(parts_of[kind], qkv if kind == "q" else wout)
        elif kind in "qw" and arg == "s":
            place_sib(parts_of[kind], qkv if kind == "q" else wout)
        elif kind in "qw":
            (qkv if kind == "q" else wout).step(arg)
        elif kind == "p":
            project(*map(int, arg))
        elif kind == "e":
            rope()
        elif kind == "a":
            attend(*map(int, arg))
        elif kind == "d":
            wait_sends(True)
        elif kind == "t":
            terms(*map(int, arg))
        else:
            ring({"g": pair, "r": relay, "f": final}[kind], *map(int, arg))

    @pl.when(away)
    def _():
        for j in range(NO):
            wait_recv(out.at[:, out_cols(j)], fsem.at[j])

    wait_sends(False)
    assert len(sends) <= N_SEND, len(sends)


def body(tokens, gain, wq, wk, wv, bq, bk, bv, wo):
    trig = rope_tables()
    any_, vm = pl.BlockSpec(memory_space=pl.ANY), pl.BlockSpec(memory_space=pltpu.VMEM)
    dma = lambda *n: pltpu.SemaphoreType.DMA(n)
    return pl.pallas_call(
        kernel,
        out_shape=jax.ShapeDtypeStruct((ROWS, WIDTH), BF16),
        in_specs=[any_, vm, any_, any_, any_, vm, vm, vm, any_, any_],
        out_specs=vm,
        scratch_shapes=[
            pltpu.VMEM((ROWS, WIDTH), BF16),
            pltpu.VMEM((ROWS, WIDTH), BF16),
            pltpu.VMEM((SEQ, WIDTH), BF16),
            pltpu.VMEM((WIDTH, WC), BF16),
            pltpu.VMEM((WIDTH, QC), BF16),
            pltpu.VMEM((SEQ, WC), F32),
            pltpu.VMEM((SEQ, QC), BF16),
            pltpu.VMEM((SEQ, HEAD), BF16),
            pltpu.VMEM((SEQ, HEAD), BF16),
            pltpu.VMEM((SEQ, QC), BF16),
            pltpu.VMEM((SEQ, HEAD), F32),
            pltpu.VMEM((QC,), F32),
            pltpu.VMEM((1, HEAD), F32),
            pltpu.VMEM((1, HEAD), F32),
            pltpu.VMEM((NO, 512, OC), BF16),
            pltpu.VMEM((NO, 2, 64, OC), BF16),
            pltpu.VMEM((NO, 4, 64, OC), BF16),
            pltpu.VMEM((NO, 4, 64, OC), F32),
            dma(8), dma(N_SEND), dma(16, 2), dma(16, 2), dma(4), dma(NK, 4), dma(NK, 4), dma(NK), dma(3),
            dma(NO), dma(NO, 2), dma(NO, 4), dma(NO),
        ],
        compiler_params=pltpu.CompilerParams(
            collective_id=0, has_side_effects=True, vmem_limit_bytes=67043328
        ),
    )(
        tokens, gain.reshape(1, -1), wq, wk, wv, bq, bk.reshape(1, -1), bv.reshape(1, -1), wo,
        jnp.asarray(trig),
    )


def solution(mesh):
    placed = (
        P(("fsdp", "sp"), None), P(), P("fsdp", "sp"), P("fsdp", "sp"), P("fsdp", "sp"),
        P("sp"), P("sp"), P("sp"), P("fsdp", "sp"),
    )
    return jax.shard_map(
        body, mesh=mesh, in_specs=placed, out_specs=P(("fsdp", "sp"), None), check_vma=False
    )
```

time: 162 us -> 143 us (0.88)
  Pallas kernels: 158 us -> 141 us
    pallas_call x1, Pallas kernels: 158 us -> 141 us  [body(): pl.pallas_call(kernel, out_shape=jax.ShapeDtypeStruct((ROWS, WIDTH), BF16...]
where the time goes in v2:
time: 143 us
  Pallas kernels  141 us (99%)
  local copies, waits for them, and re-layouts  2.46 us (2%)
    pallas_call x1, Pallas kernels, body(): pl.pallas_call(kernel, out_shape=jax.ShapeDtypeStruct((ROWS, WIDTH), BF16...  141 us

profile of v2, /device:TPU:1, one launch (start us, length us, event | category | flops | bytes accessed | tf_op | source)
XLA Modules:
  0.0 143.2 jit_solution(4240597784490202676)
XLA Ops:
  0.0 140.7 %shard_map.100 = bf16[128,5120]{1,0:T(8,128)(2,1)} custom-call(bf16[128,5120]{1,0:T(8,128)(2,1)} %tok_hbm.1, f32[1,5120]{1,0:T(1,128)} %bitcast.3, bf16[320,640]{1,0:T(8,128)(2,1)} %wq_hbm.1, bf16[320,128]{1,0:T(8,128)(2,1)} %wk_hbm.1, bf16[320,128]{1,0:T(8,128)(2,1)} %wv_hbm.1, f32[640]{0:T(1024)} %bq_in.1, f32[1,128]{1,0:T(1,128)} %bitcast.4, ...), custom_call_target="tpu_custom_call" | custom-call | tf_op jit(solution)/shard_map/pallas_call | solution.py:582
  140.7 2.5 %copy.12 = bf16[128,5120]{1,0:T(8,128)(2,1)} copy(bf16[128,5120]{1,0:T(8,128)(2,1)} %shard_map.100) | data formatting | bytes 2621440

commit v3 on v2

--- a/solution.py
+++ b/solution.py
@@ -25,18 +25,18 @@
 N_SEND = 300
 F32 = jnp.float32
 BF16 = jnp.bfloat16
-LATE_Q, OUTER_Q = 0, (0, 2)
-LATE_O, OUTER_O = 1, (0, 2, 3)
+LATE_Q, OUTER_Q = 0, (0, 1)
+LATE_O, OUTER_O = 1, (0, 1, 2, 3)
 SCHEDULE = (
-    "qo", "xw", "xo0", "qn1", "xr0", "xo1", "xo2", "qs", "qh1", "qh3", "qh2", "qn2", "xl0", "wo", "xo3", "xr1",
-    "qh4", "xr2", "qn4a", "xl1", "qh5", "xl2", "xs0", "xs1", "ws", "xr3", "qh4b", "p00", "qn4b", "qn3a", "wh1", "xs2",
-    "p01", "qn3b", "p20", "qn5", "qh7b", "xl3", "p10", "qh7a", "qh6", "p11", "p21", "qn6b", "qn6a", "xs3", "p30", "wn1",
-    "qh8", "p31", "e", "a302", "wn2", "a325", "a105", "a005", "d", "a202", "wh4b", "t00", "a225", "wn4a", "t10", "g10",
-    "g00", "r00", "wn4b", "wn3a", "wh3", "r10", "wh2", "wh4", "t12", "g12", "t14", "g14", "f00", "t02", "r12", "g02",
-    "t11", "t04", "wn5", "g11", "wn6a", "g04", "wh7a", "t16", "t01", "g01", "wh6", "wn3b", "g16", "t06", "f10", "g06",
-    "wh5", "t03", "t13", "r01", "r04", "r06", "g03", "wh7b", "t05", "r02", "wh8", "r11", "r14", "r16", "g05", "g13",
-    "t15", "wn6b", "t07", "r13", "f11", "g15", "t17", "f12", "r03", "f06", "g07", "f04", "f01", "f13", "f02", "r05",
-    "f16", "g17", "r07", "f03", "r15", "f05", "r17", "f07", "f14", "f15", "f17",
+    "qo", "n", "qn1", "xw", "xo0", "qs", "qn2", "xo1", "xo2", "qh1", "xr0", "qn4a", "qh2", "xr1", "xr2", "xo3",
+    "qh3", "qn3b", "wo", "qh4", "xl0", "xs0", "qn4b", "qh4b", "qn3a", "xl2", "p00", "xl1", "xr3", "ws", "p01", "xs2",
+    "p20", "qh6", "xs1", "qn5", "wh1", "qh5", "p11", "xl3", "p10", "qn6b", "wh2", "p21", "qh7a", "xs3", "qn6a", "p30",
+    "wn1", "qh7b", "qh8", "p31", "e", "d", "a202", "wn2", "a325", "wh3", "a302", "a225", "t10", "a005", "a105", "t00",
+    "g00", "wn4a", "g10", "wn3a", "wn4b", "t02", "wh7a", "r10", "t12", "g12", "wh4b", "t14", "wh4", "g14", "g02", "wn3b",
+    "t11", "r00", "wn5", "t04", "g11", "r02", "wn6a", "t16", "f00", "g04", "t01", "g01", "t06", "g06", "f02", "f10",
+    "wh6", "wh5", "t03", "r14", "r12", "g16", "wh8", "wn6b", "t13", "r04", "g13", "t15", "g15", "f14", "r01", "g03",
+    "t05", "wh7b", "t17", "f12", "g17", "f04", "f01", "r03", "g05", "t07", "g07", "r16", "r06", "r13", "r17", "f16",
+    "r15", "f03", "r11", "f13", "r05", "r07", "f17", "f15", "f06", "f05", "f07", "f11",
 )
 
 
@@ -154,7 +154,6 @@
         for k, (src, dst) in enumerate(((bq_in, bq), (bk_in, bk), (bv_in, bv))):
             dst[...] = src[...]
 
-    pltpu.make_async_copy(tok_hbm, tok, lsem.at[0]).wait()
     my_rows = pl.multiple_of(c * (4 * ROWS) + x * ROWS, ROWS)
 
     def norm_to(dst, base):
@@ -165,13 +164,16 @@
             ms = jnp.mean(t * t, axis=-1, keepdims=True)
             dst[pl.ds(pl.multiple_of(base + r0, 16), 16), :] = (t * lax.rsqrt(ms + 1e-06) * gain[...]).astype(BF16)
 
-    @pl.when(home)
-    def _():
-        norm_to(xb, my_rows)
-
-    @pl.when(away)
-    def _():
-        norm_to(stage, 0)
+    def norm():
+        pltpu.make_async_copy(tok_hbm, tok, lsem.at[0]).wait()
+
+        @pl.when(home)
+        def _():
+            norm_to(xb, my_rows)
+
+        @pl.when(away)
+        def _():
+            norm_to(stage, 0)
 
     pl.semaphore_wait(barrier, 7 + (c + zl) % 2)
 
@@ -555,6 +557,8 @@
             (qkv if kind == "q" else wout).step(arg)
         elif kind == "p":
             project(*map(int, arg))
+        elif kind == "n":
+            norm()
         elif kind == "e":
             rope()
         elif kind == "a":

time: 143 us -> 140 us (0.979)
  Pallas kernels: 141 us -> 137 us
    pallas_call x1, Pallas kernels: 141 us -> 137 us  [body(): pl.pallas_call(kernel, out_shape=jax.ShapeDtypeStruct((ROWS, WIDTH), BF16...]
where the time goes in v3:
time: 140 us
  Pallas kernels  137 us (98%)
  local copies, waits for them, and re-layouts  2.46 us (2%)
    pallas_call x1, Pallas kernels, body(): pl.pallas_call(kernel, out_shape=jax.ShapeDtypeStruct((ROWS, WIDTH), BF16...  137 us

profile of v3, /device:TPU:1, one launch (start us, length us, event | category | flops | bytes accessed | tf_op | source)
XLA Modules:
  0.0 139.8 jit_solution(11249055217947759504)
XLA Ops:
  0.0 137.3 %shard_map.100 = bf16[128,5120]{1,0:T(8,128)(2,1)} custom-call(bf16[128,5120]{1,0:T(8,128)(2,1)} %tok_hbm.1, f32[1,5120]{1,0:T(1,128)} %bitcast.3, bf16[320,640]{1,0:T(8,128)(2,1)} %wq_hbm.1, bf16[320,128]{1,0:T(8,128)(2,1)} %wk_hbm.1, bf16[320,128]{1,0:T(8,128)(2,1)} %wv_hbm.1, f32[640]{0:T(1024)} %bq_in.1, f32[1,128]{1,0:T(1,128)} %bitcast.4, ...), custom_call_target="tpu_custom_call" | custom-call | tf_op jit(solution)/shard_map/pallas_call | solution.py:586
  137.3 2.5 %copy.12 = bf16[128,5120]{1,0:T(8,128)(2,1)} copy(bf16[128,5120]{1,0:T(8,128)(2,1)} %shard_map.100) | data formatting | bytes 2621440

commit v4 on v3

--- a/solution.py
+++ b/solution.py
@@ -26,7 +26,7 @@
 F32 = jnp.float32
 BF16 = jnp.bfloat16
 LATE_Q, OUTER_Q = 0, (0, 1)
-LATE_O, OUTER_O = 1, (0, 1, 2, 3)
+LATE_O, OUTER_O = 1, (0, 2, 3)
 SCHEDULE = (
     "qo", "n", "qn1", "xw", "xo0", "qs", "qn2", "xo1", "xo2", "qh1", "xr0", "qn4a", "qh2", "xr1", "xr2", "xo3",
     "qh3", "qn3b", "wo", "qh4", "xl0", "xs0", "qn4b", "qh4b", "qn3a", "xl2", "p00", "xl1", "xr3", "ws", "p01", "xs2",

time: 140 us -> 140 us (level)
  no operation moved by 1% of the time
where the time goes in v4:
time: 140 us
  Pallas kernels  137 us (98%)
  local copies, waits for them, and re-layouts  2.46 us (2%)
    pallas_call x1, Pallas kernels, body(): pl.pallas_call(kernel, out_shape=jax.ShapeDtypeStruct((ROWS, WIDTH), BF16...  137 us

profile of v4, /device:TPU:1, one launch (start us, length us, event | category | flops | bytes accessed | tf_op | source)
XLA Modules:
  0.0 139.8 jit_solution(3841010619226469283)
XLA Ops:
  0.0 137.3 %shard_map.100 = bf16[128,5120]{1,0:T(8,128)(2,1)} custom-call(bf16[128,5120]{1,0:T(8,128)(2,1)} %tok_hbm.1, f32[1,5120]{1,0:T(1,128)} %bitcast.3, bf16[320,640]{1,0:T(8,128)(2,1)} %wq_hbm.1, bf16[320,128]{1,0:T(8,128)(2,1)} %wk_hbm.1, bf16[320,128]{1,0:T(8,128)(2,1)} %wv_hbm.1, f32[640]{0:T(1024)} %bq_in.1, f32[1,128]{1,0:T(1,128)} %bitcast.4, ...), custom_call_target="tpu_custom_call" | custom-call | tf_op jit(solution)/shard_map/pallas_call | solution.py:586
  137.3 2.5 %copy.12 = bf16[128,5120]{1,0:T(8,128)(2,1)} copy(bf16[128,5120]{1,0:T(8,128)(2,1)} %shard_map.100) | data formatting | bytes 2621440
